TPU v7x, 1024 devices: a whole 8x8x8 slice. The times are simulated.
1024 devices in a mesh: ctx: 64 (over y_lo, x, core), tp: 16 (over y_hi, z).
Axes of the slice: x: 8, y: 8 (y_hi: 2, y_lo: 4; y = y_hi * 4 + y_lo), z: 8, core: 2. Of those that a mesh axis runs over, the one named last changes fastest.
Arguments:
- out_grad: bfloat16 [16384, 8192], P(('ctx', 'tp')), may hold values from -6 to 6
- saved_input: bfloat16 [16384, 8192], P(('ctx', 'tp')), may hold values from -6 to 6
- explicit_filter_weights: float32 [128, 8192], P(None, 'tp'), may hold values from -0.5 to 0.5
- gate_taps: float32 [3, 8192], P(None, 'tp'), may hold values from -3.5 to 3.5
- value_featurizer_weights: float32 [3, 8192], P(None, 'tp'), may hold values from -3.5 to 3.5
Outputs:
- input_grad: bfloat16 [16384, 8192], P('ctx', 'tp')
- explicit_filter_gradient: float32 [128, 8192], P(None, 'tp')
- gate_grad: float32 [3, 8192], P(None, 'tp')
- value_grad: float32 [3, 8192], P(None, 'tp')
All inputs are finite; a program needn't handle non-finite values.
Results may differ from a plain program's by a relative error of at most 0.004.
Values may be sent and summed in bfloat16 or wider, within the bound.
A program may use at most 32 MiB of HBM per device.

v0:
```python
import math

import jax
import jax.numpy as jnp
from jax import lax
from jax.sharding import PartitionSpec as P


def for_sending(x):

    def short(part):
        return part.astype(jnp.bfloat16) if part.dtype == jnp.float32 else part

    return jax.tree.map(short, x)


def from_behind(x, axis, by):
    count = lax.axis_size(axis)
    pairs = [(i, i + by) for i in range(count) if 0 <= i + by < count]
    return lax.ppermute(x, axis, pairs)


def depthwise(signal, kernel):
    channels = signal.shape[1]
    result = lax.conv_general_dilated(
        signal[None],
        kernel[:, None, :],
        (1,),
        "VALID",
        dimension_numbers=("NWC", "WIO", "NWC"),
        feature_group_count=channels,
        precision=lax.Precision.HIGHEST,
    )
    return result[0]


def causal_mixing(padded, taps, count):
    filter_extent = taps.shape[0]
    return depthwise(padded[: count + filter_extent - 1], taps[::-1])


def anticausal(padded, taps, count):
    return depthwise(padded[: count + taps.shape[0] - 1], taps)


def delayed_input(left, right, filter_extent, base):
    count = left.shape[0]
    start = base - filter_extent + 1
    segment = right[start : start + count + filter_extent - 1]
    return depthwise(segment, left)[::-1]


def compose(value_featurizer_weights, explicit_filter_weights):
    short = value_featurizer_weights.shape[0]
    filter_extent = explicit_filter_weights.shape[0]
    total = jnp.zeros((filter_extent + short - 1, explicit_filter_weights.shape[1]), jnp.float32)
    for i in range(short):
        total = total.at[i : i + filter_extent].add(
            value_featurizer_weights[i] * explicit_filter_weights
        )
    return total


def pass_back(head):
    return from_behind(for_sending(head), "ctx", -1).astype(head.dtype)


def shards(out_grad, saved_input, explicit_filter_weights, gate_taps, value_featurizer_weights):
    tp_count = lax.axis_size("tp")
    width = out_grad.shape[1] // tp_count
    token_rows = out_grad.shape[0] * tp_count
    filter_extent = explicit_filter_weights.shape[0]
    short = gate_taps.shape[0]
    reach = filter_extent + short - 2
    stacked = jnp.stack([out_grad, saved_input])
    local = lax.all_to_all(stacked, "tp", split_axis=2, concat_axis=1, tiled=True)
    input_bf = local[1]
    tail = from_behind(input_bf[token_rows - reach :], "ctx", 1)
    grad_f = local[0].astype(jnp.float32)
    extended_input = jnp.concatenate([tail, input_bf]).astype(jnp.float32)
    extended_value = causal_mixing(
        extended_input, value_featurizer_weights, token_rows + filter_extent - 1
    )
    qext = causal_mixing(extended_input, gate_taps, token_rows + filter_extent - 1)
    gate = qext[filter_extent - 1 :]
    pext = causal_mixing(extended_input, explicit_filter_weights, token_rows + short - 1)
    mixed_signal = causal_mixing(extended_value, explicit_filter_weights, token_rows)
    grad_q = grad_f * mixed_signal
    mixed_signal_gradient = grad_f * gate
    combined = compose(value_featurizer_weights, explicit_filter_weights)
    zpad = jnp.concatenate(
        [
            jnp.zeros((reach, width), jnp.float32),
            mixed_signal_gradient,
            jnp.zeros((reach, width), jnp.float32),
        ]
    )
    qpad = jnp.concatenate(
        [jnp.zeros((reach, width), jnp.float32), grad_q, jnp.zeros((short - 1, width), jnp.float32)]
    )
    whole = anticausal(zpad, combined, token_rows + reach) + anticausal(
        qpad, gate_taps, token_rows + reach
    )
    head = whole[:reach]
    own_rows = whole[reach:]
    incoming = pass_back(head)
    input_grad = jnp.concatenate(
        [own_rows[: token_rows - reach], own_rows[token_rows - reach :] + incoming]
    ).astype(jnp.bfloat16)
    gradient_scale = jnp.float32(1.0 / math.sqrt(token_rows * lax.axis_size("ctx")))
    explicit_filter_term = (
        delayed_input(mixed_signal_gradient, extended_value, filter_extent, filter_extent - 1)
        * gradient_scale
    )
    gate_part = delayed_input(grad_q, extended_input, short, reach) * gradient_scale
    value_part = delayed_input(mixed_signal_gradient, pext, short, short - 1) * gradient_scale
    explicit_filter_gradient, gate_grad, value_grad = lax.psum(
        (explicit_filter_term, gate_part, value_part), "ctx"
    )
    return (input_grad, explicit_filter_gradient, gate_grad, value_grad)


def solution(mesh):
    placed = (
        P(("ctx", "tp"), None),
        P(("ctx", "tp"), None),
        P(None, "tp"),
        P(None, "tp"),
        P(None, "tp"),
    )
    return jax.shard_map(
        shards,
        mesh=mesh,
        in_specs=placed,
        out_specs=(P("ctx", "tp"), P(None, "tp"), P(None, "tp"), P(None, "tp")),
        check_vma=False,
    )
```

profile of v0, /device:TPU:1, one launch (start us, length us, event | category | flops | bytes accessed | tf_op | source)
XLA Modules:
  0.0 632.3 jit_solution(12339782228683674039)
XLA Ops:
  7.2 1.1 pad_maximum_fusion.1
  8.2 6.7 %copy.100 = bf16[2,16,8192]{1,0,2:T(2,128)(2,1)} copy(bf16[2,16,8192]{2,1,0:T(8,128)(2,1)S(1)} %pad_maximum_fusion.1) | data formatting | bytes 1048576 | tf_op jit(solution)/shard_map/stack | solution.py:75
  14.9 6.4 %reshape.165 = bf16[16,2,8192]{2,1,0:T(2,128)(2,1)} reshape(bf16[8192,2,16]{2,1,0:T(2,128)(2,1)} %bitcast.67) | data formatting | bytes 1048576
  21.4 23.2 %all-to-all-start = ((bf16[16,2,8192]{2,1,0:T(2,128)(2,1)}), bf16[16,2,8192]{2,1,0:T(2,128)(2,1)S(1)}, u32[]{:S(2)}, u32[]{:S(2)}) async-start(bf16[16,2,8192]{2,1,0:T(2,128)(2,1)} %reshape.165), calls=%async_computation | async-start | bytes 1048576 | tf_op jit(solution)/shard_map/all_to_all | solution.py:76
  45.7 14.3 %all-to-all-done = bf16[16,2,8192]{2,1,0:T(2,128)(2,1)S(1)} async-done(((bf16[16,2,8192]{2,1,0:T(2,128)(2,1)}), bf16[16,2,8192]{2,1,0:T(2,128)(2,1)S(1)}, u32[]{:S(2)}, u32[]{:S(2)}) %all-to-all-start) | async-done | bytes 524320 | tf_op jit(solution)/shard_map/all_to_all | solution.py:76
  60.0 4.1 reshape.166
  64.1 8.9 %copy.101 = bf16[2,16,16,512]{3,1,2,0:T(8,128)(2,1)S(1)} copy(bf16[2,16,16,512]{1,0,3,2:T(2,128)(2,1)} %bitcast.68) | data formatting | bytes 1048576 | tf_op jit(solution)/shard_map/all_to_all | solution.py:76
  73.0 5.7 collective-permute-start
  79.2 0.7 copy-done.2
  79.9 0.7 collective-permute-done
  80.6 0.6 copy-done.7
  82.2 0.5 copy.110
  82.7 1.9 reshape.163
  84.6 5.9 fusion.5
  90.5 5.3 fusion.38
  97.0 1.1 bitcast_multiply_fusion
  98.6 1.0 reshape.145
  99.6 0.6 copy-done.13
  100.4 0.5 copy.116
  100.9 1.9 reshape.164
  102.9 0.7 broadcast_in_dim.41
  104.1 8.4 %convolution_add_fusion = f32[1,385,512]{2,0,1:T(1,128)S(1)} fusion(f32[1,514,512]{2,0,1:T(1,128)S(1)} %broadcast_in_dim.41, f32[1,392,512]{2,0,1:T(1,128)S(1)} %copy-done.6, f32[130,1,512]{2,0,1:T(8,128)S(1)} %copy-done.3), kind=kOutput, calls=%fused_computation.3 | convolution fusion | flops 307704320 | bytes 2895872 | tf_op jit(solution)/shard_map/conv_general_dilated | solution.py:25
  112.6 1.3 copy-done.5
  114.1 5.3 fusion.29
  119.4 1.3 fusion.27
  120.9 1.0 fusion.8
  122.2 2.1 collective-permute-start.1
  124.4 0.7 broadcast_multiply_fusion
  125.2 262.7 %all-reduce.1 = (f32[3,512]{1,0:T(4,128)}, f32[3,512]{1,0:T(4,128)}) all-reduce(f32[3,512]{1,0:T(4,128)S(1)} %get-tuple-element.50, f32[3,512]{1,0:T(4,128)S(1)} %get-tuple-element.49), channel_id=1, replica_groups=mesh['ctx'=64,'tp'=16] {'ctx'}, use_global_device_ids=true, to_apply=%region_1.0 | all-reduce | flops 3072 | bytes 24576 | tf_op jit(solution)/shard_map/psum | solution.py:117
  388.0 0.7 pad_maximum_fusion.3
  388.7 235.0 %all-reduce.4.cloned.1.call-done = f32[128,512]{1,0:T(8,128)} async-done(((f32[128,512]{1,0:T(8,128)}), f32[128,512]{1,0:T(8,128)}) %all-reduce.4.cloned.1.call-update) | async-done | bytes 262160 | tf_op jit(solution)/shard_map/psum | solution.py:117
  623.8 1.7 copy.168
  (82 shorter events, 5.8 us)
Async XLA Ops:
  14.9 29.7 %copy-start.11 = (f32[3,512]{1,0:T(4,128)S(1)}, f32[3,512]{1,0:T(4,128)}, u32[]{:S(2)}) copy-start(f32[3,512]{1,0:T(4,128)} %param.15) | copy-start | bytes 18436
  21.4 23.4 %copy-start = (f32[128,512]{1,0:T(8,128)S(1)}, f32[128,512]{1,0:T(8,128)}, u32[]{:S(2)}) copy-start(f32[128,512]{1,0:T(8,128)} %param.13) | copy-start | bytes 786436
  21.4 23.6 %copy-start.12 = (f32[3,512]{1,0:T(4,128)S(1)}, f32[3,512]{1,0:T(4,128)}, u32[]{:S(2)}) copy-start(f32[3,512]{1,0:T(4,128)} %param.14) | copy-start | bytes 18436
  21.4 38.6 %all-to-all-start = ((bf16[16,2,8192]{2,1,0:T(2,128)(2,1)}), bf16[16,2,8192]{2,1,0:T(2,128)(2,1)S(1)}, u32[]{:S(2)}, u32[]{:S(2)}) async-start(bf16[16,2,8192]{2,1,0:T(2,128)(2,1)} %reshape.165), calls=%async_computation | async-start | bytes 1048576 | tf_op jit(solution)/shard_map/all_to_all | solution.py:76
  44.6 579.2 %all-reduce.4.cloned.1.call-start = ((), (), s32[]{:S(2)}) async-start(), calls=%async_computation.1 | async-start | bytes 524288 | tf_op jit(solution)/shard_map/psum | solution.py:117
  73.0 7.5 %collective-permute-start = (bf16[129,512]{1,0:T(8,128)(2,1)S(1)}, bf16[129,512]{1,0:T(8,128)(2,1)S(1)}, u32[]{:S(2)}, u32[]{:S(2)}) collective-permute-start(bf16[129,512]{1,0:T(8,128)(2,1)S(1)} %slice.135), channel_id=1, source_target_pairs={{0,16},{16,32},{32,48},{48,64},{64,80},{80,96},{96,112},{112,128},... | collective-permute-start | bytes 396296 | tf_op jit(solution)/shard_map/ppermute | solution.py:20
  79.2 0.7 copy-start.2
  80.6 0.7 copy-start.7
  81.3 0.7 copy-start.14
  84.6 5.9 copy-start.4
  95.8 0.7 copy-start.15
  99.5 0.7 copy-start.13
  102.9 1.0 copy-start.3
  102.9 1.2 copy-start.6
  112.5 6.8 %copy-start.1 = (f32[1,385,512]{2,0,1:T(1,128)}, f32[1,385,512]{2,0,1:T(1,128)S(1)}, u32[]{:S(2)}) copy-start(f32[1,385,512]{2,0,1:T(1,128)S(1)} %convolution_add_fusion) | copy-start | bytes 2365444
  112.6 1.4 copy-start.5
  112.6 1.6 copy-start.10
  114.1 5.3 copy-start.16
  119.4 1.4 copy-start.8
  119.4 1.5 copy-start.9
  122.1 265.8 %slice-start = ((f32[1,385,512]{2,0,1:T(1,128)}), f32[1,129,512]{2,0,1:T(1,128)S(1)}, s32[]{:S(2)}) async-start(f32[1,385,512]{2,0,1:T(1,128)} %copy-done.1), calls=%async_computation.2 | async-start | bytes 528384 | tf_op jit(solution)/shard_map/slice | solution.py:108
  122.2 265.8 %collective-permute-start.1 = (bf16[129,512]{1,0:T(8,128)(2,1)S(1)}, bf16[129,512]{1,0:T(8,128)(2,1)S(1)}, u32[]{:S(2)}, u32[]{:S(2)}) collective-permute-start(bf16[129,512]{1,0:T(8,128)(2,1)S(1)} %slice_bitcast_fusion), channel_id=1, source_target_pairs={{16,0},{32,16},{48,32},{64,48},{80,64},{96,80},{112,96},{128,112},... | collective-permute-start | bytes 396296 | tf_op jit(solution)/shard_map/ppermute | solution.py:20
Sparse Core Ops, SparseCore 0:
  125.3 498.4 all-reduce.3
where the time goes:
time: 633 us; the launch traced here: 632 us
  blocking collectives  263 us (42%)
  waiting for transfers between devices  250 us (39%)
  local copies, waits for them, and re-layouts  41.9 us (7%)
  starting transfers between devices  31 us (5%)
  matrix products  27.7 us (4%)
  between operations  14.6 us (2%)
    psum x1, blocking collectives, shards(): lax.psum((explicit_filter_term, gate_part, value_part), 'ctx')  263 us
    psum x1, waiting for transfers between devices, shards(): lax.psum((explicit_filter_term, gate_part, value_part), 'ctx')  235 us
    conv_general_dilated x8, matrix products, depthwise(): lax.conv_general_dilated(signal[None], kernel[:, None, :], (1,), 'VALID',...  27.5 us
    all_to_all x1, starting transfers between devices, shards(): lax.all_to_all(stacked, 'tp', split_axis=2, concat_axis=1, tiled=True)  23.2 us
    unnamed x40, local copies, waits for them, and re-layouts  17 us
    all_to_all x1, waiting for transfers between devices, shards(): lax.all_to_all(stacked, 'tp', split_axis=2, concat_axis=1, tiled=True)  14.3 us
  transfers between devices with their start and end apart: 4, of which 3 were waited for; matrix products, arithmetic and copies ran while one was open for 0% of the time, Pallas kernels for 0%

commit v1 on v0

v1 whole, which is shorter than its diff:
```python
import functools
import math

import jax
import jax.numpy as jnp
import ml_dtypes
import numpy as np
from jax import lax
from jax.experimental import pallas as pl
from jax.experimental.pallas import tpu as pltpu
from jax.sharding import PartitionSpec as P

MESH = pl.DeviceIdType.MESH
F32 = jnp.float32
BF16 = jnp.bfloat16
EXTRA = 8


def two_parts(matrix):
    high = matrix.astype(ml_dtypes.bfloat16)
    low = (matrix - high.astype(np.float64)).astype(ml_dtypes.bfloat16)
    return high, low


def transforms(length):
    odd = 2 * np.arange(length // 2)[:, None] + 1
    steps = (odd * np.arange(length)[None, :]) % (2 * length)
    angle = np.pi * steps / length
    forward = np.concatenate([np.cos(angle), -np.sin(angle)])
    inverse = forward.T * (2.0 / length)
    return two_parts(forward) + two_parts(inverse)


def split(x):
    high = x.astype(BF16)
    return high, (x - high.astype(F32)).astype(BF16)


def dot3(ah, al, xh, xl):
    def dot(a, b):
        return jnp.dot(a, b, preferred_element_type=F32)

    return dot(ah, xh) + dot(ah, xl) + dot(al, xh)


def kernel(
    sizes,
    og, si, h_hbm, gt_ref, w_ref, fh_hbm, fl_hbm, ih_hbm, il_hbm,
    ig_out, efg_out, gate_out, value_out,
    ubuf, gbuf, hb, fh, fl, ih, il,
    hs, vs, ds, uf, qb, zb, xh, xl, w1b, dqb, igb, head, head_in,
    part, part_in, ext, rs, xr, yr, ag, ext_in,
    a2a_send, a2a_recv, halo_send, halo_recv, head_send, head_recv,
    const_sem, one_send, one_recv,
):
    nctx, ntp, xs, ys, taps, scale = sizes
    rows, width = og.shape[0], og.shape[1] // ntp
    tokens = rows * ntp
    chans = width // 2
    halo = ubuf.shape[1] - tokens
    length = tokens + taps
    half_len = length // 2
    slice_rows = taps // xs
    ctx, tp = lax.axis_index("ctx"), lax.axis_index("tp")
    core = lax.rem(ctx, 2)
    x = lax.rem(ctx // 2, xs)
    ylo = ctx // (2 * xs)
    row16 = lax.rem(ctx, 2 * xs)

    def remote(src, dst, send, recv, to_ctx, to_tp):
        return pltpu.make_async_remote_copy(
            src_ref=src, dst_ref=dst, send_sem=send, recv_sem=recv,
            device_id=(to_ctx, to_tp), device_id_type=MESH,
        )

    def finish(ref, sem):
        pltpu.make_async_copy(ref, ref, sem).wait()

    def offset(k):
        half = (1 - core) if k == 0 else core
        return pl.multiple_of(half * chans, chans)

    def tp_peer(i):
        return lax.rem(tp + i, ntp)

    def row_peer(i):
        return ylo * (2 * xs) + lax.rem(row16 + i, 2 * xs)

    def x_peer(i):
        return lax.rem(x + i, xs)

    def x_ctx(other):
        return (ylo * xs + other) * 2 + core

    def y_ctx(i):
        return (lax.rem(ylo + i, ys) * xs + x) * 2 + core

    barrier = pltpu.get_barrier_semaphore()

    def greet(to_ctx, to_tp):
        pl.semaphore_signal(barrier, inc=1, device_id=(to_ctx, to_tp), device_id_type=MESH)

    def loop(count, body):
        def step(i, carry):
            body(i)
            return carry

        lax.fori_loop(1, count, step, 0)

    loop(ntp, lambda i: greet(ctx, tp_peer(i)))
    loop(2 * xs, lambda i: greet(row_peer(i), tp))
    loop(ys, lambda i: greet(y_ctx(i), tp))

    @pl.when(ctx > 0)
    def _():
        greet(ctx - 1, tp)

    @pl.when(ctx < nctx - 1)
    def _():
        greet(ctx + 1, tp)

    constants = [
        pltpu.make_async_copy(src, dst, const_sem.at[i])
        for i, (src, dst) in enumerate(
            [(fh_hbm, fh), (fl_hbm, fl), (ih_hbm, ih), (il_hbm, il)]
            + [(h_hbm.at[:, pl.ds(offset(k), chans)], hb.at[k]) for k in range(2)]
        )
    ]
    for copy in constants:
        copy.start()

    @pl.when(ctx == 0)
    def _():
        ubuf[:, 0:halo, :] = jnp.zeros((2, halo, chans), BF16)

    @pl.when(ctx == nctx - 1)
    def _():
        head_in[...] = jnp.zeros(head_in.shape, BF16)

    greeted = ntp - 1 + 2 * xs - 1 + ys - 1
    greeted = greeted + jnp.where(ctx > 0, 1, 0) + jnp.where(ctx < nctx - 1, 1, 0)
    pl.semaphore_wait(barrier, greeted)

    def exchange(src, dst, base, k, sem):
        def columns(who):
            return src.at[:, pl.ds(pl.multiple_of(who * width + offset(k), chans), chans)]

        place = dst.at[k, pl.ds(pl.multiple_of(base + tp * rows, 16), rows), :]
        loop(
            ntp,
            lambda i: remote(
                columns(tp_peer(i)), place, a2a_send.at[sem], a2a_recv.at[sem], ctx, tp_peer(i)
            ).start(),
        )
        pltpu.make_async_copy(columns(tp), place, a2a_recv.at[sem]).start()

    exchange(si, ubuf, halo, 0, 0)
    exchange(si, ubuf, halo, 1, 1)
    exchange(og, gbuf, 0, 0, 2)
    exchange(og, gbuf, 0, 1, 3)

    for copy in constants:
        copy.wait()
    for k in range(2):
        th, tl = split(hb[k])
        hs[k] = dot3(fh[:, 0:taps], fl[:, 0:taps], th, tl)
    w1b[:, 0:16, :] = jnp.zeros((2, 16, chans), F32)
    w1b[:, 16 + length : 32 + length, :] = jnp.zeros((2, 16, chans), F32)
    dqb[:, 0:16, :] = jnp.zeros((2, 16, chans), F32)
    dqb[:, 16 + tokens : 32 + tokens, :] = jnp.zeros((2, 16, chans), F32)

    def taps_of(ref, k):
        block = ref[:, pl.ds(offset(k), chans)]
        return [block[i : i + 1] for i in range(3)]

    def halo_copy(k):
        return remote(
            ubuf.at[k, pl.ds(tokens, halo), :], ubuf.at[1 - k, pl.ds(0, halo), :],
            halo_send.at[k], halo_recv.at[1 - k], ctx + 1, tp,
        )

    for k in range(2):
        finish(ubuf.at[k, pl.ds(halo, tokens), :], a2a_recv.at[k])

        @pl.when(ctx < nctx - 1)
        def _(k=k):
            halo_copy(k).start()

    def spectrum_product(a, a_k, b, b_k, sign):
        for r in range(0, half_len, 32):
            ar, ai = a[a_k, r : r + 32], a[a_k, half_len + r : half_len + r + 32]
            br, bi = b[b_k, r : r + 32], b[b_k, half_len + r : half_len + r + 32]
            if sign > 0:
                re, im = ar * br - ai * bi, ar * bi + ai * br
            else:
                re, im = ar * br + ai * bi, ar * bi - ai * br
            xh[r : r + 32], xl[r : r + 32] = split(re)
            xh[half_len + r : half_len + r + 32], xl[half_len + r : half_len + r + 32] = split(im)

    def delayed(k, r, count):
        first = halo - taps + r
        return [uf[k, first - i : first - i + count] for i in range(3)]

    for k in range(2):

        @pl.when(ctx > 0)
        def _(k=k):
            finish(ubuf.at[k, pl.ds(0, halo), :], halo_recv.at[k])

        for r in range(0, halo + tokens, 16):
            uf[k, r : r + 16] = ubuf[k, r : r + 16].astype(F32)
        wv, wg = taps_of(w_ref, k), taps_of(gt_ref, k)
        for r in range(0, length, 32):
            u = delayed(k, r, 32)
            v = wv[0] * u[0] + wv[1] * u[1] + wv[2] * u[2]
            xh[r : r + 32], xl[r : r + 32] = split(v)
            if r >= taps:
                qb[k, r - taps : r - taps + 32] = wg[0] * u[0] + wg[1] * u[1] + wg[2] * u[2]
        vs[k] = dot3(fh[...], fl[...], xh[...], xl[...])
        spectrum_product(hs, k, vs, k, 1)
        zb[k] = dot3(ih[taps:, :], il[taps:, :], xh[...], xl[...])

    def fold(values):
        return jnp.sum(values.reshape(values.shape[0] // 8, 8, chans), axis=0)

    def input_gradient(k):
        wv, wg = taps_of(w_ref, k), taps_of(gt_ref, k)
        for r in range(0, halo + tokens, 16):
            a = [w1b[k, r + i : r + i + 16] for i in range(3)]
            total = wv[0] * a[0] + wv[1] * a[1] + wv[2] * a[2]
            first = r - halo
            if first >= -16:
                d = [dqb[k, 16 + first + i : 32 + first + i] for i in range(3)]
                total = total + wg[0] * d[0] + wg[1] * d[1] + wg[2] * d[2]
            if first < 0:
                head[k, r : r + 16] = total.astype(BF16)
            else:
                igb[k, first : first + 16] = total

        @pl.when(ctx > 0)
        def _():
            remote(
                head.at[k], head_in.at[1 - k], head_send.at[k], head_recv.at[1 - k], ctx - 1, tp
            ).start()

    partner = ctx + 1 - 2 * core

    for k in range(2):
        finish(gbuf.at[k], a2a_recv.at[2 + k])
        gate_sums = [jnp.zeros((8, chans), F32) for _ in range(3)]
        for r in range(0, tokens, 32):
            g = gbuf[k, r : r + 32].astype(F32)
            xh[taps + r : taps + r + 32], xl[taps + r : taps + r + 32] = split(
                g * qb[k, r : r + 32]
            )
            dq = g * zb[k, r : r + 32]
            dqb[k, 16 + r : 48 + r] = dq
            u = delayed(k, taps + r, 32)
            gate_sums = [s + fold(dq * d) for s, d in zip(gate_sums, u)]
        ds[0] = dot3(fh[:, taps:], fl[:, taps:], xh[taps:, :], xl[taps:, :])
        spectrum_product(hs, k, ds, 0, -1)
        w1b[k, 16 : 16 + length] = dot3(ih[...], il[...], xh[...], xl[...])
        value_sums = [jnp.zeros((8, chans), F32) for _ in range(3)]
        for r in range(0, length, 32):
            w1 = w1b[k, 16 + r : 48 + r]
            u = delayed(k, r, 32)
            value_sums = [s + fold(w1 * d) for s, d in zip(value_sums, u)]
        for i, s in enumerate(gate_sums + value_sums):
            ext[i : i + 1] = jnp.sum(s, axis=0, keepdims=True) * scale
        ext[6:8] = jnp.zeros((2, chans), F32)
        spectrum_product(vs, k, ds, 0, -1)
        part[0:taps] = dot3(ih[0:taps, :], il[0:taps, :], xh[...], xl[...]) * scale
        part[taps : taps + EXTRA] = ext[...]
        if k == 0:
            sent = remote(part, part_in, one_send.at[0], one_recv.at[0], partner, tp)
            sent.start()
            input_gradient(k)
            sent.wait_send()

    finish(part_in, one_recv.at[0])
    extra_total = part[taps : taps + EXTRA] + part_in[taps : taps + EXTRA]
    for s in range(xs):
        rows_of = slice(s * slice_rows, (s + 1) * slice_rows)
        rs[s, 0:slice_rows] = part[rows_of] + part_in[rows_of]
        rs[s, slice_rows : slice_rows + EXTRA] = extra_total
    loop(
        xs,
        lambda i: remote(
            rs.at[x_peer(i)], xr.at[x], one_send.at[1], one_recv.at[1], x_ctx(x_peer(i)), tp
        ).start(),
    )
    xr[x] = rs[x]
    input_gradient(1)
    finish(xr.at[pl.ds(0, xs - 1)], one_recv.at[1])
    total = xr[0]
    for s in range(1, xs):
        total = total + xr[s]
    yr[ylo] = total
    loop(
        ys,
        lambda i: remote(
            yr.at[ylo], yr.at[ylo], one_send.at[2], one_recv.at[2], y_ctx(i), tp
        ).start(),
    )

    @pl.when(ctx < nctx - 1)
    def _():
        for k in range(2):
            finish(head_in.at[k], head_recv.at[k])

    for k in range(2):
        for r in range(0, tokens, 16):
            block = igb[k, r : r + 16]
            late = r - (tokens - halo)
            if late >= 0:
                block = block + head_in[k, late : late + 16].astype(F32)
            ig_out[r : r + 16, pl.ds(offset(k), chans)] = block.astype(BF16)

    finish(yr.at[pl.ds(0, ys - 1)], one_recv.at[2])
    total = yr[0]
    for s in range(1, ys):
        total = total + yr[s]
    slot = core * xs + x
    ag[slot] = total[0:slice_rows]
    ext[...] = total[slice_rows : slice_rows + EXTRA]
    loop(
        2 * xs,
        lambda i: remote(
            ag.at[slot], ag.at[slot], one_send.at[3], one_recv.at[3], row_peer(i), tp
        ).start(),
    )
    remote(ext, ext_in, one_send.at[4], one_recv.at[4], partner, tp).start()
    gate_out[:, pl.ds(offset(1), chans)] = ext[0:3]
    value_out[:, pl.ds(offset(1), chans)] = ext[3:6]
    finish(ext_in, one_recv.at[4])
    gate_out[:, pl.ds(offset(0), chans)] = ext_in[0:3]
    value_out[:, pl.ds(offset(0), chans)] = ext_in[3:6]
    finish(ag.at[pl.ds(0, 2 * xs - 1)], one_recv.at[3])
    for half in range(2):
        for s in range(xs):
            efg_out[
                s * slice_rows : (s + 1) * slice_rows, half * chans : (half + 1) * chans
            ] = ag[half * xs + s]

    for k in range(2):
        finish(ubuf.at[k, pl.ds(0, rows * (ntp - 1)), :], a2a_send.at[k])
        finish(gbuf.at[k, pl.ds(0, rows * (ntp - 1)), :], a2a_send.at[2 + k])

        @pl.when(ctx < nctx - 1)
        def _(k=k):
            finish(ubuf.at[k, pl.ds(0, halo), :], halo_send.at[k])

        @pl.when(ctx > 0)
        def _(k=k):
            finish(head.at[k], head_send.at[k])

    finish(rs.at[pl.ds(0, xs - 1)], one_send.at[1])
    finish(yr.at[pl.ds(0, ys - 1)], one_send.at[2])
    finish(ag.at[pl.ds(0, 2 * xs - 1)], one_send.at[3])
    finish(ext, one_send.at[4])


def shards(mesh, out_grad, saved_input, explicit_filter_weights, gate_taps, value_featurizer_weights):
    nctx, ntp = mesh.shape["ctx"], mesh.shape["tp"]
    rows, channels = out_grad.shape
    width = channels // ntp
    tokens = rows * ntp
    taps = explicit_filter_weights.shape[0]
    xs = 8 if nctx >= 64 else 2
    ys = nctx // (2 * xs)
    chans = width // 2
    halo = -(-(taps + gate_taps.shape[0] - 2) // 16) * 16
    length = tokens + taps
    slice_rows = taps // xs
    scale = np.float32(1.0 / math.sqrt(tokens * nctx))
    matrices = [jnp.asarray(m) for m in transforms(length)]
    anywhere = pl.BlockSpec(memory_space=pl.ANY)
    vmem = pl.BlockSpec(memory_space=pltpu.VMEM)
    scratch = [
        pltpu.VMEM((2, halo + tokens, chans), BF16),
        pltpu.VMEM((2, tokens, chans), BF16),
        pltpu.VMEM((2, taps, chans), F32),
        *[pltpu.VMEM((length, length), BF16) for _ in range(4)],
        pltpu.VMEM((2, length, chans), F32),
        pltpu.VMEM((2, length, chans), F32),
        pltpu.VMEM((1, length, chans), F32),
        pltpu.VMEM((2, halo + tokens, chans), F32),
        pltpu.VMEM((2, tokens, chans), F32),
        pltpu.VMEM((2, tokens, chans), F32),
        pltpu.VMEM((length, chans), BF16),
        pltpu.VMEM((length, chans), BF16),
        pltpu.VMEM((2, length + 32, chans), F32),
        pltpu.VMEM((2, tokens + 32, chans), F32),
        pltpu.VMEM((2, tokens, chans), F32),
        pltpu.VMEM((2, halo, chans), BF16),
        pltpu.VMEM((2, halo, chans), BF16),
        pltpu.VMEM((taps + EXTRA, chans), F32),
        pltpu.VMEM((taps + EXTRA, chans), F32),
        pltpu.VMEM((EXTRA, chans), F32),
        pltpu.VMEM((xs, slice_rows + EXTRA, chans), F32),
        pltpu.VMEM((xs, slice_rows + EXTRA, chans), F32),
        pltpu.VMEM((ys, slice_rows + EXTRA, chans), F32),
        pltpu.VMEM((2 * xs, slice_rows, chans), F32),
        pltpu.VMEM((EXTRA, chans), F32),
        pltpu.SemaphoreType.DMA((4,)),
        pltpu.SemaphoreType.DMA((4,)),
        pltpu.SemaphoreType.DMA((2,)),
        pltpu.SemaphoreType.DMA((2,)),
        pltpu.SemaphoreType.DMA((2,)),
        pltpu.SemaphoreType.DMA((2,)),
        pltpu.SemaphoreType.DMA((6,)),
        pltpu.SemaphoreType.DMA((5,)),
        pltpu.SemaphoreType.DMA((5,)),
    ]
    return pl.pallas_call(
        functools.partial(kernel, (nctx, ntp, xs, ys, taps, scale)),
        out_shape=(
            jax.ShapeDtypeStruct((tokens, width), BF16),
            jax.ShapeDtypeStruct((taps, width), F32),
            jax.ShapeDtypeStruct(gate_taps.shape, F32),
            jax.ShapeDtypeStruct(value_featurizer_weights.shape, F32),
        ),
        in_specs=[anywhere, anywhere, anywhere, vmem, vmem] + [anywhere] * 4,
        out_specs=(vmem, vmem, vmem, vmem),
        scratch_shapes=scratch,
        compiler_params=pltpu.CompilerParams(
            collective_id=0, has_side_effects=True, vmem_limit_bytes=48 * 2**20
        ),
    )(
        out_grad, saved_input, explicit_filter_weights, gate_taps, value_featurizer_weights,
        *matrices,
    )


def solution(mesh):
    placed = (
        P(("ctx", "tp"), None),
        P(("ctx", "tp"), None),
        P(None, "tp"),
        P(None, "tp"),
        P(None, "tp"),
    )
    return jax.shard_map(
        functools.partial(shards, mesh),
        mesh=mesh,
        in_specs=placed,
        out_specs=(P("ctx", "tp"), P(None, "tp"), P(None, "tp"), P(None, "tp")),
        check_vma=False,
    )
```

time: 633 us -> 73.5 us (0.12)
  blocking collectives: 263 us -> 0 us
  waiting for transfers between devices: 250 us -> 0 us
  Pallas kernels: 0 us -> 61.7 us
  local copies, waits for them, and re-layouts: 41.9 us -> 10.7 us
  starting transfers between devices: 31 us -> 0 us
  matrix products: 27.7 us -> 0 us
  between operations: 14.6 us -> 0.66 us
    psum x1 -> x0, blocking collectives: 263 us -> none  [shards(): lax.psum((explicit_filter_term, gate_part, value_part), 'ctx')]
    psum x1 -> x0, waiting for transfers between devices: 235 us -> none  [shards(): lax.psum((explicit_filter_term, gate_part, value_part), 'ctx')]
    pallas_call x0 -> x1, Pallas kernels: none -> 61.7 us  [shards(): pl.pallas_call(functools.partial(kernel, (nctx, ntp, xs, ys, taps, scale)...]
    conv_general_dilated x8 -> x0, matrix products: 27.5 us -> none  [depthwise(): lax.conv_general_dilated(signal[None], kernel[:, None, :], (1,), 'VALID',...]
    all_to_all x1 -> x0, starting transfers between devices: 23.2 us -> none  [shards(): lax.all_to_all(stacked, 'tp', split_axis=2, concat_axis=1, tiled=True)]
    all_to_all x1 -> x0, waiting for transfers between devices: 14.3 us -> none  [shards(): lax.all_to_all(stacked, 'tp', split_axis=2, concat_axis=1, tiled=True)]
    all_to_all x1 -> x0, local copies, waits for them, and re-layouts: 8.9 us -> none  [shards(): lax.all_to_all(stacked, 'tp', split_axis=2, concat_axis=1, tiled=True)]
    ppermute x2 -> x0, starting transfers between devices: 7.75 us -> none  [from_behind(): return lax.ppermute(x, axis, pairs)]
  transfers between devices with their start and end apart: 4 -> 0, of which waited for: 3 -> 0; matrix products, arithmetic and copies ran while one was open for 0% -> 0% of each run, Pallas kernels for 0% -> 0%
where the time goes in v1:
time: 73.5 us; the launch traced here: 73.1 us
  Pallas kernels  61.7 us (84%)
  local copies, waits for them, and re-layouts  10.7 us (15%)
    pallas_call x1, Pallas kernels, shards(): pl.pallas_call(functools.partial(kernel, (nctx, ntp, xs, ys, taps, scale)...  61.7 us
    unnamed x22, local copies, waits for them, and re-layouts  10.7 us

profile of v1, /device:TPU:1, one launch (start us, length us, event | category | flops | bytes accessed | tf_op | source)
XLA Modules:
  0.0 73.1 jit_solution(16419310978348565635)
XLA Ops:
  0.6 0.0 copy-start
  0.6 1.0 %copy-done = bf16[384,384]{1,0:T(8,128)(2,1)S(1)} copy-done((bf16[384,384]{1,0:T(8,128)(2,1)S(1)}, bf16[384,384]{1,0:T(8,128)(2,1)}, u32[]{:S(2)}) %copy-start) | copy-done | bytes 294936
  1.6 0.0 copy-start.1
  1.6 1.0 %copy-done.1 = bf16[384,384]{1,0:T(8,128)(2,1)S(1)} copy-done((bf16[384,384]{1,0:T(8,128)(2,1)S(1)}, bf16[384,384]{1,0:T(8,128)(2,1)}, u32[]{:S(2)}) %copy-start.1) | copy-done | bytes 294936
  2.6 0.0 copy-start.2
  2.6 1.0 %copy-done.2 = bf16[384,384]{1,0:T(8,128)(2,1)S(1)} copy-done((bf16[384,384]{1,0:T(8,128)(2,1)S(1)}, bf16[384,384]{1,0:T(8,128)(2,1)}, u32[]{:S(2)}) %copy-start.2) | copy-done | bytes 294936
  3.5 0.0 copy-start.3
  3.5 1.0 %copy-done.3 = bf16[384,384]{1,0:T(8,128)(2,1)S(1)} copy-done((bf16[384,384]{1,0:T(8,128)(2,1)S(1)}, bf16[384,384]{1,0:T(8,128)(2,1)}, u32[]{:S(2)}) %copy-start.3) | copy-done | bytes 294936
  4.5 0.0 copy-start.4
  4.5 0.9 %copy-done.4 = bf16[16,8192]{1,0:T(8,128)(2,1)S(1)} copy-done((bf16[16,8192]{1,0:T(8,128)(2,1)S(1)}, bf16[16,8192]{1,0:T(8,128)(2,1)}, u32[]{:S(2)}) %copy-start.4) | copy-done | bytes 262168
  5.4 0.0 copy-start.5
  5.4 0.9 %copy-done.5 = bf16[16,8192]{1,0:T(8,128)(2,1)S(1)} copy-done((bf16[16,8192]{1,0:T(8,128)(2,1)S(1)}, bf16[16,8192]{1,0:T(8,128)(2,1)}, u32[]{:S(2)}) %copy-start.5) | copy-done | bytes 262168
  6.4 0.0 copy-start.6
  6.4 0.9 %copy-done.6 = f32[128,512]{1,0:T(8,128)S(1)} copy-done((f32[128,512]{1,0:T(8,128)S(1)}, f32[128,512]{1,0:T(8,128)}, u32[]{:S(2)}) %copy-start.6) | copy-done | bytes 262168
  7.3 0.0 copy-start.7
  7.3 0.7 copy-done.7
  8.0 0.0 copy-start.8
  8.0 0.7 copy-done.8
  8.7 61.7 %shard_map.120 = (bf16[256,512]{1,0:T(8,128)(2,1)S(1)}, f32[128,512]{1,0:T(8,128)S(1)}, f32[3,512]{1,0:T(4,128)S(1)}, f32[3,512]{1,0:T(4,128)S(1)}) custom-call(bf16[16,8192]{1,0:T(8,128)(2,1)S(1)} %copy-done.4, bf16[16,8192]{1,0:T(8,128)(2,1)S(1)} %copy-done.5, f32[128,512]{1,0:T(8,128)S(1)} %copy-done.6, f32[3,512]{1,0:T(4,128)S(1)} %copy-done.7, ...), custom_call_target="tpu_custom_call" | custom-call | tf_op jit(solution)/shard_map/pallas_call | solution.py:415
  70.5 0.7 copy.17
  71.2 0.7 copy.18
  71.9 0.6 copy.19
  72.5 0.6 copy.20
Async XLA Ops:
  0.6 1.0 %copy-start = (bf16[384,384]{1,0:T(8,128)(2,1)S(1)}, bf16[384,384]{1,0:T(8,128)(2,1)}, u32[]{:S(2)}) copy-start(bf16[384,384]{1,0:T(8,128)(2,1)} %constant.11.clone.il_hbm) | copy-start | bytes 884740
  1.6 1.0 %copy-start.1 = (bf16[384,384]{1,0:T(8,128)(2,1)S(1)}, bf16[384,384]{1,0:T(8,128)(2,1)}, u32[]{:S(2)}) copy-start(bf16[384,384]{1,0:T(8,128)(2,1)} %constant.10.clone.ih_hbm) | copy-start | bytes 884740
  2.6 1.0 %copy-start.2 = (bf16[384,384]{1,0:T(8,128)(2,1)S(1)}, bf16[384,384]{1,0:T(8,128)(2,1)}, u32[]{:S(2)}) copy-start(bf16[384,384]{1,0:T(8,128)(2,1)} %constant.9.clone.fl_hbm) | copy-start | bytes 884740
  3.5 1.0 %copy-start.3 = (bf16[384,384]{1,0:T(8,128)(2,1)S(1)}, bf16[384,384]{1,0:T(8,128)(2,1)}, u32[]{:S(2)}) copy-start(bf16[384,384]{1,0:T(8,128)(2,1)} %constant.8.clone.fh_hbm) | copy-start | bytes 884740
  4.5 0.9 %copy-start.4 = (bf16[16,8192]{1,0:T(8,128)(2,1)S(1)}, bf16[16,8192]{1,0:T(8,128)(2,1)}, u32[]{:S(2)}) copy-start(bf16[16,8192]{1,0:T(8,128)(2,1)} %og.1) | copy-start | bytes 786436
  5.4 0.9 %copy-start.5 = (bf16[16,8192]{1,0:T(8,128)(2,1)S(1)}, bf16[16,8192]{1,0:T(8,128)(2,1)}, u32[]{:S(2)}) copy-start(bf16[16,8192]{1,0:T(8,128)(2,1)} %si.1) | copy-start | bytes 786436
  6.4 0.9 %copy-start.6 = (f32[128,512]{1,0:T(8,128)S(1)}, f32[128,512]{1,0:T(8,128)}, u32[]{:S(2)}) copy-start(f32[128,512]{1,0:T(8,128)} %h_hbm.1) | copy-start | bytes 786436
  7.3 0.7 copy-start.7
  8.0 0.7 copy-start.8

commit v2 on v1

--- a/solution.py
+++ b/solution.py
@@ -45,11 +45,11 @@
 
 def kernel(
     sizes,
-    og, si, h_hbm, gt_ref, w_ref, fh_hbm, fl_hbm, ih_hbm, il_hbm,
+    og, si, h_hbm, gt_hbm, w_hbm, fh_hbm, fl_hbm, ih_hbm, il_hbm,
     ig_out, efg_out, gate_out, value_out,
     ubuf, gbuf, hb, fh, fl, ih, il,
     hs, vs, ds, uf, qb, zb, xh, xl, w1b, dqb, igb, head, head_in,
-    part, part_in, ext, rs, xr, yr, ag, ext_in,
+    part, part_in, ext, rs, xr, yr, ag, ext_in, gt_ref, w_ref,
     a2a_send, a2a_recv, halo_send, halo_recv, head_send, head_recv,
     const_sem, one_send, one_recv,
 ):
@@ -122,7 +122,7 @@
     constants = [
         pltpu.make_async_copy(src, dst, const_sem.at[i])
         for i, (src, dst) in enumerate(
-            [(fh_hbm, fh), (fl_hbm, fl), (ih_hbm, ih), (il_hbm, il)]
+            [(fh_hbm, fh), (fl_hbm, fl), (ih_hbm, ih), (il_hbm, il), (gt_hbm, gt_ref), (w_hbm, w_ref)]
             + [(h_hbm.at[:, pl.ds(offset(k), chans)], hb.at[k]) for k in range(2)]
         )
     ]
@@ -360,6 +360,16 @@
     finish(ext, one_send.at[4])
 
 
+def write_out(*refs):
+    copies = [
+        pltpu.make_async_copy(refs[i], refs[4 + i], refs[8].at[i]) for i in range(4)
+    ]
+    for copy in copies:
+        copy.start()
+    for copy in copies:
+        copy.wait()
+
+
 def shards(mesh, out_grad, saved_input, explicit_filter_weights, gate_taps, value_featurizer_weights):
     nctx, ntp = mesh.shape["ctx"], mesh.shape["tp"]
     rows, channels = out_grad.shape
@@ -374,7 +384,7 @@
     slice_rows = taps // xs
     scale = np.float32(1.0 / math.sqrt(tokens * nctx))
     matrices = [jnp.asarray(m) for m in transforms(length)]
-    anywhere = pl.BlockSpec(memory_space=pl.ANY)
+    hbm = pl.BlockSpec(memory_space=pltpu.HBM)
     vmem = pl.BlockSpec(memory_space=pltpu.VMEM)
     scratch = [
         pltpu.VMEM((2, halo + tokens, chans), BF16),
@@ -402,17 +412,19 @@
         pltpu.VMEM((ys, slice_rows + EXTRA, chans), F32),
         pltpu.VMEM((2 * xs, slice_rows, chans), F32),
         pltpu.VMEM((EXTRA, chans), F32),
+        pltpu.VMEM(gate_taps.shape, F32),
+        pltpu.VMEM(value_featurizer_weights.shape, F32),
         pltpu.SemaphoreType.DMA((4,)),
         pltpu.SemaphoreType.DMA((4,)),
         pltpu.SemaphoreType.DMA((2,)),
         pltpu.SemaphoreType.DMA((2,)),
         pltpu.SemaphoreType.DMA((2,)),
         pltpu.SemaphoreType.DMA((2,)),
-        pltpu.SemaphoreType.DMA((6,)),
+        pltpu.SemaphoreType.DMA((8,)),
         pltpu.SemaphoreType.DMA((5,)),
         pltpu.SemaphoreType.DMA((5,)),
     ]
-    return pl.pallas_call(
+    results = pl.pallas_call(
         functools.partial(kernel, (nctx, ntp, xs, ys, taps, scale)),
         out_shape=(
             jax.ShapeDtypeStruct((tokens, width), BF16),
@@ -420,16 +432,24 @@
             jax.ShapeDtypeStruct(gate_taps.shape, F32),
             jax.ShapeDtypeStruct(value_featurizer_weights.shape, F32),
         ),
-        in_specs=[anywhere, anywhere, anywhere, vmem, vmem] + [anywhere] * 4,
+        in_specs=[hbm] * 9,
         out_specs=(vmem, vmem, vmem, vmem),
         scratch_shapes=scratch,
         compiler_params=pltpu.CompilerParams(
-            collective_id=0, has_side_effects=True, vmem_limit_bytes=48 * 2**20
+            collective_id=0, has_side_effects=True, vmem_limit_bytes=55_900_000
         ),
     )(
         out_grad, saved_input, explicit_filter_weights, gate_taps, value_featurizer_weights,
         *matrices,
     )
+    return pl.pallas_call(
+        write_out,
+        out_shape=[jax.ShapeDtypeStruct(r.shape, r.dtype) for r in results],
+        in_specs=[vmem] * 4,
+        out_specs=[hbm] * 4,
+        scratch_shapes=[pltpu.SemaphoreType.DMA((4,))],
+        compiler_params=pltpu.CompilerParams(vmem_limit_bytes=2**20),
+    )(*results)
 
 
 def solution(mesh):

time: 73.5 us -> 65 us (0.88)
  local copies, waits for them, and re-layouts: 10.7 us -> 1.39 us
  Pallas kernels: 61.7 us -> 62.8 us
    unnamed x22 -> x4, local copies, waits for them, and re-layouts: 10.7 us -> 1.39 us
    pallas_call x0 -> x1, Pallas kernels: none -> 0.83 us  [shards(): pl.pallas_call(write_out, out_shape=[jax.ShapeDtypeStruct(r.shape, r.dtyp...]
where the time goes in v2:
time: 65 us; the launch traced here: 64.8 us
  Pallas kernels  62.8 us (97%)
  local copies, waits for them, and re-layouts  1.39 us (2%)
  between operations  0.65 us (1%)
    pallas_call x1, Pallas kernels, shards(): pl.pallas_call(functools.partial(kernel, (nctx, ntp, xs, ys, taps, scale)...  61.9 us
    unnamed x4, local copies, waits for them, and re-layouts  1.39 us

profile of v2, /device:TPU:1, one launch (start us, length us, event | category | flops | bytes accessed | tf_op | source)
XLA Modules:
  0.0 64.8 jit_solution(1443207512587603347)
XLA Ops:
  0.6 0.0 copy-start
  0.6 0.7 %copy-done = f32[3,512]{1,0:T(4,128)S(1)} copy-done((f32[3,512]{1,0:T(4,128)S(1)}, f32[3,512]{1,0:T(4,128)}, u32[]{:S(2)}) %copy-start) | copy-done | bytes 6168
  1.3 0.0 copy-start.1
  1.3 0.7 %copy-done.1 = f32[3,512]{1,0:T(4,128)S(1)} copy-done((f32[3,512]{1,0:T(4,128)S(1)}, f32[3,512]{1,0:T(4,128)}, u32[]{:S(2)}) %copy-start.1) | copy-done | bytes 6168
  2.0 61.9 %shard_map.120 = (bf16[256,512]{1,0:T(8,128)(2,1)S(1)}, f32[128,512]{1,0:T(8,128)S(1)}, f32[3,512]{1,0:T(4,128)S(1)}, f32[3,512]{1,0:T(4,128)S(1)}) custom-call(bf16[16,8192]{1,0:T(8,128)(2,1)} %og.1, bf16[16,8192]{1,0:T(8,128)(2,1)} %si.1, f32[128,512]{1,0:T(8,128)} %h_hbm.1, f32[3,512]{1,0:T(4,128)S(1)} %copy-done, f32[3,512]{1,0:T(4,128)S(1)} %copy-done.1, ...), custom_call_target="tpu_custom_call" | custom-call | tf_op jit(solution)/shard_map/pallas_call | solution.py:427
  64.0 0.8 %shard_map.121 = (bf16[256,512]{1,0:T(8,128)(2,1)}, f32[128,512]{1,0:T(8,128)}, f32[3,512]{1,0:T(4,128)}, f32[3,512]{1,0:T(4,128)}) custom-call(bf16[256,512]{1,0:T(8,128)(2,1)S(1)} %get-tuple-element.8.refs_0_, f32[128,512]{1,0:T(8,128)S(1)} %get-tuple-element.9.refs_1_, f32[3,512]{1,0:T(4,128)S(1)} %get-tuple-element.10.refs_2_, ...), custom_call_target="tpu_custom_call" | custom-call | tf_op jit(solution)/shard_map/pallas_call | solution.py:445
Async XLA Ops:
  0.6 0.7 %copy-start = (f32[3,512]{1,0:T(4,128)S(1)}, f32[3,512]{1,0:T(4,128)}, u32[]{:S(2)}) copy-start(f32[3,512]{1,0:T(4,128)} %gt_hbm.1) | copy-start | bytes 18436
  1.3 0.7 %copy-start.1 = (f32[3,512]{1,0:T(4,128)S(1)}, f32[3,512]{1,0:T(4,128)}, u32[]{:S(2)}) copy-start(f32[3,512]{1,0:T(4,128)} %w_hbm.1) | copy-start | bytes 18436

commit v3 on v2

--- a/solution.py
+++ b/solution.py
@@ -49,7 +49,7 @@
     ig_out, efg_out, gate_out, value_out,
     ubuf, gbuf, hb, fh, fl, ih, il,
     hs, vs, ds, uf, qb, zb, xh, xl, w1b, dqb, igb, head, head_in,
-    part, part_in, ext, rs, xr, yr, ag, ext_in, gt_ref, w_ref,
+    part, part_in, ext, ext_in, rs, xr, xe, yr, ye, ag, gt_ref, w_ref,
     a2a_send, a2a_recv, halo_send, halo_recv, head_send, head_recv,
     const_sem, one_send, one_recv,
 ):
@@ -258,6 +258,21 @@
             u = delayed(k, taps + r, 32)
             gate_sums = [s + fold(dq * d) for s, d in zip(gate_sums, u)]
         ds[0] = dot3(fh[:, taps:], fl[:, taps:], xh[taps:, :], xl[taps:, :])
+        spectrum_product(vs, k, ds, 0, -1)
+        part[0:taps] = dot3(ih[0:taps, :], il[0:taps, :], xh[...], xl[...]) * scale
+        if k == 1:
+            finish(part_in, one_recv.at[0])
+            for s in range(xs):
+                rows_of = slice(s * slice_rows, (s + 1) * slice_rows)
+                rs[s] = (part[rows_of] + part_in[rows_of]).astype(BF16)
+            loop(
+                xs,
+                lambda i: remote(
+                    rs.at[x_peer(i)], xr.at[x], one_send.at[1], one_recv.at[1],
+                    x_ctx(x_peer(i)), tp,
+                ).start(),
+            )
+            xr[x] = rs[x]
         spectrum_product(hs, k, ds, 0, -1)
         w1b[k, 16 : 16 + length] = dot3(ih[...], il[...], xh[...], xl[...])
         value_sums = [jnp.zeros((8, chans), F32) for _ in range(3)]
@@ -266,40 +281,43 @@
             u = delayed(k, r, 32)
             value_sums = [s + fold(w1 * d) for s, d in zip(value_sums, u)]
         for i, s in enumerate(gate_sums + value_sums):
-            ext[i : i + 1] = jnp.sum(s, axis=0, keepdims=True) * scale
-        ext[6:8] = jnp.zeros((2, chans), F32)
-        spectrum_product(vs, k, ds, 0, -1)
-        part[0:taps] = dot3(ih[0:taps, :], il[0:taps, :], xh[...], xl[...]) * scale
-        part[taps : taps + EXTRA] = ext[...]
+            part[taps + i : taps + i + 1] = jnp.sum(s, axis=0, keepdims=True) * scale
+        part[taps + 6 : taps + 8] = jnp.zeros((2, chans), F32)
         if k == 0:
             sent = remote(part, part_in, one_send.at[0], one_recv.at[0], partner, tp)
             sent.start()
             input_gradient(k)
             sent.wait_send()
 
-    finish(part_in, one_recv.at[0])
-    extra_total = part[taps : taps + EXTRA] + part_in[taps : taps + EXTRA]
-    for s in range(xs):
-        rows_of = slice(s * slice_rows, (s + 1) * slice_rows)
-        rs[s, 0:slice_rows] = part[rows_of] + part_in[rows_of]
-        rs[s, slice_rows : slice_rows + EXTRA] = extra_total
+    own_extra = part[taps : taps + EXTRA] + part_in[taps : taps + EXTRA]
+    xe[x] = jnp.concatenate([own_extra[:, : chans // 2], own_extra[:, chans // 2 :]]).astype(BF16)
     loop(
         xs,
         lambda i: remote(
-            rs.at[x_peer(i)], xr.at[x], one_send.at[1], one_recv.at[1], x_ctx(x_peer(i)), tp
+            xe.at[x], xe.at[x], one_send.at[4], one_recv.at[4], x_ctx(x_peer(i)), tp
         ).start(),
     )
-    xr[x] = rs[x]
     input_gradient(1)
     finish(xr.at[pl.ds(0, xs - 1)], one_recv.at[1])
-    total = xr[0]
+    total = xr[0].astype(F32)
     for s in range(1, xs):
-        total = total + xr[s]
+        total = total + xr[s].astype(F32)
     yr[ylo] = total
     loop(
         ys,
         lambda i: remote(
             yr.at[ylo], yr.at[ylo], one_send.at[2], one_recv.at[2], y_ctx(i), tp
+        ).start(),
+    )
+    finish(xe.at[pl.ds(0, xs - 1)], one_recv.at[4])
+    total = xe[0].astype(F32)
+    for s in range(1, xs):
+        total = total + xe[s].astype(F32)
+    ye[ylo] = total
+    loop(
+        ys,
+        lambda i: remote(
+            ye.at[ylo], ye.at[ylo], one_send.at[5], one_recv.at[5], y_ctx(i), tp
         ).start(),
     )
 
@@ -321,26 +339,35 @@
     for s in range(1, ys):
         total = total + yr[s]
     slot = core * xs + x
-    ag[slot] = total[0:slice_rows]
-    ext[...] = total[slice_rows : slice_rows + EXTRA]
+    ag[slot] = total.astype(BF16)
     loop(
         2 * xs,
         lambda i: remote(
             ag.at[slot], ag.at[slot], one_send.at[3], one_recv.at[3], row_peer(i), tp
         ).start(),
     )
-    remote(ext, ext_in, one_send.at[4], one_recv.at[4], partner, tp).start()
-    gate_out[:, pl.ds(offset(1), chans)] = ext[0:3]
-    value_out[:, pl.ds(offset(1), chans)] = ext[3:6]
-    finish(ext_in, one_recv.at[4])
-    gate_out[:, pl.ds(offset(0), chans)] = ext_in[0:3]
-    value_out[:, pl.ds(offset(0), chans)] = ext_in[3:6]
+    finish(ye.at[pl.ds(0, ys - 1)], one_recv.at[5])
+    total = ye[0]
+    for s in range(1, ys):
+        total = total + ye[s]
+    ext[...] = total
+    remote(ext, ext_in, one_send.at[6], one_recv.at[6], partner, tp).start()
+
+    def put_extra(source, k):
+        for lane in range(2):
+            place = pl.ds(pl.multiple_of(offset(k) + lane * (chans // 2), chans // 2), chans // 2)
+            gate_out[:, place] = source[8 * lane : 8 * lane + 3]
+            value_out[:, place] = source[8 * lane + 3 : 8 * lane + 6]
+
+    put_extra(ext, 1)
+    finish(ext_in, one_recv.at[6])
+    put_extra(ext_in, 0)
     finish(ag.at[pl.ds(0, 2 * xs - 1)], one_recv.at[3])
     for half in range(2):
         for s in range(xs):
             efg_out[
                 s * slice_rows : (s + 1) * slice_rows, half * chans : (half + 1) * chans
-            ] = ag[half * xs + s]
+            ] = ag[half * xs + s].astype(F32)
 
     for k in range(2):
         finish(ubuf.at[k, pl.ds(0, rows * (ntp - 1)), :], a2a_send.at[k])
@@ -357,7 +384,9 @@
     finish(rs.at[pl.ds(0, xs - 1)], one_send.at[1])
     finish(yr.at[pl.ds(0, ys - 1)], one_send.at[2])
     finish(ag.at[pl.ds(0, 2 * xs - 1)], one_send.at[3])
-    finish(ext, one_send.at[4])
+    finish(xe.at[pl.ds(0, xs - 1)], one_send.at[4])
+    finish(ye.at[pl.ds(0, ys - 1)], one_send.at[5])
+    finish(ext, one_send.at[6])
 
 
 def write_out(*refs):
@@ -406,12 +435,14 @@
         pltpu.VMEM((2, halo, chans), BF16),
         pltpu.VMEM((taps + EXTRA, chans), F32),
         pltpu.VMEM((taps + EXTRA, chans), F32),
-        pltpu.VMEM((EXTRA, chans), F32),
-        pltpu.VMEM((xs, slice_rows + EXTRA, chans), F32),
-        pltpu.VMEM((xs, slice_rows + EXTRA, chans), F32),
-        pltpu.VMEM((ys, slice_rows + EXTRA, chans), F32),
-        pltpu.VMEM((2 * xs, slice_rows, chans), F32),
-        pltpu.VMEM((EXTRA, chans), F32),
+        pltpu.VMEM((2 * EXTRA, chans // 2), F32),
+        pltpu.VMEM((2 * EXTRA, chans // 2), F32),
+        pltpu.VMEM((xs, slice_rows, chans), BF16),
+        pltpu.VMEM((xs, slice_rows, chans), BF16),
+        pltpu.VMEM((xs, 2 * EXTRA, chans // 2), BF16),
+        pltpu.VMEM((ys, slice_rows, chans), F32),
+        pltpu.VMEM((ys, 2 * EXTRA, chans // 2), F32),
+        pltpu.VMEM((2 * xs, slice_rows, chans), BF16),
         pltpu.VMEM(gate_taps.shape, F32),
         pltpu.VMEM(value_featurizer_weights.shape, F32),
         pltpu.SemaphoreType.DMA((4,)),
@@ -421,8 +452,8 @@
         pltpu.SemaphoreType.DMA((2,)),
         pltpu.SemaphoreType.DMA((2,)),
         pltpu.SemaphoreType.DMA((8,)),
-        pltpu.SemaphoreType.DMA((5,)),
-        pltpu.SemaphoreType.DMA((5,)),
+        pltpu.SemaphoreType.DMA((7,)),
+        pltpu.SemaphoreType.DMA((7,)),
     ]
     results = pl.pallas_call(
         functools.partial(kernel, (nctx, ntp, xs, ys, taps, scale)),

time: 65 us -> 62.1 us (0.955)
  Pallas kernels: 62.8 us -> 59.8 us
    pallas_call x1, Pallas kernels: 61.9 us -> 59 us  [shards(): pl.pallas_call(functools.partial(kernel, (nctx, ntp, xs, ys, taps, scale)...]
where the time goes in v3:
time: 62.1 us; the launch traced here: 61.9 us
  Pallas kernels  59.8 us (96%)
  local copies, waits for them, and re-layouts  1.39 us (2%)
  between operations  0.65 us (1%)
    pallas_call x1, Pallas kernels, shards(): pl.pallas_call(functools.partial(kernel, (nctx, ntp, xs, ys, taps, scale)...  59 us
    unnamed x4, local copies, waits for them, and re-layouts  1.39 us

profile of v3, /device:TPU:1, one launch (start us, length us, event | category | flops | bytes accessed | tf_op | source)
XLA Modules:
  0.0 61.9 jit_solution(15171999220377883486)
XLA Ops:
  0.6 0.0 copy-start
  0.6 0.7 %copy-done = f32[3,512]{1,0:T(4,128)S(1)} copy-done((f32[3,512]{1,0:T(4,128)S(1)}, f32[3,512]{1,0:T(4,128)}, u32[]{:S(2)}) %copy-start) | copy-done | bytes 6168
  1.3 0.0 copy-start.1
  1.3 0.7 %copy-done.1 = f32[3,512]{1,0:T(4,128)S(1)} copy-done((f32[3,512]{1,0:T(4,128)S(1)}, f32[3,512]{1,0:T(4,128)}, u32[]{:S(2)}) %copy-start.1) | copy-done | bytes 6168
  2.0 59.0 %shard_map.120 = (bf16[256,512]{1,0:T(8,128)(2,1)S(1)}, f32[128,512]{1,0:T(8,128)S(1)}, f32[3,512]{1,0:T(4,128)S(1)}, f32[3,512]{1,0:T(4,128)S(1)}) custom-call(bf16[16,8192]{1,0:T(8,128)(2,1)} %og.1, bf16[16,8192]{1,0:T(8,128)(2,1)} %si.1, f32[128,512]{1,0:T(8,128)} %h_hbm.1, f32[3,512]{1,0:T(4,128)S(1)} %copy-done, f32[3,512]{1,0:T(4,128)S(1)} %copy-done.1, ...), custom_call_target="tpu_custom_call" | custom-call | tf_op jit(solution)/shard_map/pallas_call | solution.py:458
  61.0 0.8 %shard_map.121 = (bf16[256,512]{1,0:T(8,128)(2,1)}, f32[128,512]{1,0:T(8,128)}, f32[3,512]{1,0:T(4,128)}, f32[3,512]{1,0:T(4,128)}) custom-call(bf16[256,512]{1,0:T(8,128)(2,1)S(1)} %get-tuple-element.8.refs_0_, f32[128,512]{1,0:T(8,128)S(1)} %get-tuple-element.9.refs_1_, f32[3,512]{1,0:T(4,128)S(1)} %get-tuple-element.10.refs_2_, ...), custom_call_target="tpu_custom_call" | custom-call | tf_op jit(solution)/shard_map/pallas_call | solution.py:476
Async XLA Ops:
  0.6 0.7 %copy-start = (f32[3,512]{1,0:T(4,128)S(1)}, f32[3,512]{1,0:T(4,128)}, u32[]{:S(2)}) copy-start(f32[3,512]{1,0:T(4,128)} %gt_hbm.1) | copy-start | bytes 18436
  1.3 0.7 %copy-start.1 = (f32[3,512]{1,0:T(4,128)S(1)}, f32[3,512]{1,0:T(4,128)}, u32[]{:S(2)}) copy-start(f32[3,512]{1,0:T(4,128)} %w_hbm.1) | copy-start | bytes 18436

commit v4 on v3

--- a/solution.py
+++ b/solution.py
@@ -49,7 +49,7 @@
     ig_out, efg_out, gate_out, value_out,
     ubuf, gbuf, hb, fh, fl, ih, il,
     hs, vs, ds, uf, qb, zb, xh, xl, w1b, dqb, igb, head, head_in,
-    part, part_in, ext, ext_in, rs, xr, xe, yr, ye, ag, gt_ref, w_ref,
+    uh, part, part_in, ep, ep_in, ext, ext_in, rs, xr, xe, yr, ye, ag, gt_ref, w_ref,
     a2a_send, a2a_recv, halo_send, halo_recv, head_send, head_recv,
     const_sem, one_send, one_recv,
 ):
@@ -65,7 +65,11 @@
     core = lax.rem(ctx, 2)
     x = lax.rem(ctx // 2, xs)
     ylo = ctx // (2 * xs)
-    row16 = lax.rem(ctx, 2 * xs)
+    deep = ntp // 2
+    tp_far = sorted(range(deep), key=lambda d: -min(d, deep - d))
+    tp_order = [(far, d) for d in tp_far for far in (1, 0) if far or d]
+    x_order = sorted(range(1, xs), key=lambda d: -min(d, xs - d))
+    row_order = [(d, c) for d in x_order for c in range(2)] + [(0, 1)]
 
     def remote(src, dst, send, recv, to_ctx, to_tp):
         return pltpu.make_async_remote_copy(
@@ -80,14 +84,16 @@
         half = (1 - core) if k == 0 else core
         return pl.multiple_of(half * chans, chans)
 
-    def tp_peer(i):
-        return lax.rem(tp + i, ntp)
-
-    def row_peer(i):
-        return ylo * (2 * xs) + lax.rem(row16 + i, 2 * xs)
-
-    def x_peer(i):
-        return lax.rem(x + i, xs)
+    def tp_peer(step):
+        far, d = step
+        return lax.rem(tp // deep + far, 2) * deep + lax.rem(lax.rem(tp, deep) + d, deep)
+
+    def x_peer(d):
+        return lax.rem(x + d, xs)
+
+    def row_peer(step):
+        d, c = step
+        return (ylo * xs + x_peer(d)) * 2 + lax.rem(core + c, 2)
 
     def x_ctx(other):
         return (ylo * xs + other) * 2 + core
@@ -100,16 +106,12 @@
     def greet(to_ctx, to_tp):
         pl.semaphore_signal(barrier, inc=1, device_id=(to_ctx, to_tp), device_id_type=MESH)
 
-    def loop(count, body):
-        def step(i, carry):
-            body(i)
-            return carry
-
-        lax.fori_loop(1, count, step, 0)
-
-    loop(ntp, lambda i: greet(ctx, tp_peer(i)))
-    loop(2 * xs, lambda i: greet(row_peer(i), tp))
-    loop(ys, lambda i: greet(y_ctx(i), tp))
+    for step in tp_order:
+        greet(ctx, tp_peer(step))
+    for step in row_order:
+        greet(row_peer(step), tp)
+    for i in range(1, ys):
+        greet(y_ctx(i), tp)
 
     @pl.when(ctx > 0)
     def _():
@@ -146,12 +148,9 @@
             return src.at[:, pl.ds(pl.multiple_of(who * width + offset(k), chans), chans)]
 
         place = dst.at[k, pl.ds(pl.multiple_of(base + tp * rows, 16), rows), :]
-        loop(
-            ntp,
-            lambda i: remote(
-                columns(tp_peer(i)), place, a2a_send.at[sem], a2a_recv.at[sem], ctx, tp_peer(i)
-            ).start(),
-        )
+        for step in tp_order:
+            to = tp_peer(step)
+            remote(columns(to), place, a2a_send.at[sem], a2a_recv.at[sem], ctx, to).start()
         pltpu.make_async_copy(columns(tp), place, a2a_recv.at[sem]).start()
 
     exchange(si, ubuf, halo, 0, 0)
@@ -178,13 +177,6 @@
             ubuf.at[k, pl.ds(tokens, halo), :], ubuf.at[1 - k, pl.ds(0, halo), :],
             halo_send.at[k], halo_recv.at[1 - k], ctx + 1, tp,
         )
-
-    for k in range(2):
-        finish(ubuf.at[k, pl.ds(halo, tokens), :], a2a_recv.at[k])
-
-        @pl.when(ctx < nctx - 1)
-        def _(k=k):
-            halo_copy(k).start()
 
     def spectrum_product(a, a_k, b, b_k, sign):
         for r in range(0, half_len, 32):
@@ -197,26 +189,46 @@
             xh[r : r + 32], xl[r : r + 32] = split(re)
             xh[half_len + r : half_len + r + 32], xl[half_len + r : half_len + r + 32] = split(im)
 
-    def delayed(k, r, count):
+    def delayed(ref, k, r, count):
         first = halo - taps + r
-        return [uf[k, first - i : first - i + count] for i in range(3)]
-
-    for k in range(2):
-
+        return [ref[k, first - i : first - i + count] for i in range(3)]
+
+    def mixed(weights, signals):
+        return weights[0] * signals[0] + weights[1] * signals[1] + weights[2] * signals[2]
+
+    def own_spectrum(k):
+        finish(ubuf.at[k, pl.ds(halo, tokens), :], a2a_recv.at[k])
+
+        @pl.when(ctx < nctx - 1)
+        def _():
+            halo_copy(k).start()
+
+        wv, wg = taps_of(w_ref, k), taps_of(gt_ref, k)
+        for r in range(halo, halo + tokens, 32):
+            uf[k, r : r + 32] = ubuf[k, r : r + 32].astype(F32)
+        for r in range(taps, length, 32):
+            u = delayed(uf, k, r, 32)
+            xh[r : r + 32], xl[r : r + 32] = split(mixed(wv, u))
+            qb[k, r - taps : r - taps + 32] = mixed(wg, u)
+        vs[k] = dot3(fh[:, taps:], fl[:, taps:], xh[taps:, :], xl[taps:, :])
+
+    def halo_spectrum(k):
         @pl.when(ctx > 0)
-        def _(k=k):
+        def _():
             finish(ubuf.at[k, pl.ds(0, halo), :], halo_recv.at[k])
 
-        for r in range(0, halo + tokens, 16):
-            uf[k, r : r + 16] = ubuf[k, r : r + 16].astype(F32)
         wv, wg = taps_of(w_ref, k), taps_of(gt_ref, k)
-        for r in range(0, length, 32):
-            u = delayed(k, r, 32)
-            v = wv[0] * u[0] + wv[1] * u[1] + wv[2] * u[2]
-            xh[r : r + 32], xl[r : r + 32] = split(v)
-            if r >= taps:
-                qb[k, r - taps : r - taps + 32] = wg[0] * u[0] + wg[1] * u[1] + wg[2] * u[2]
-        vs[k] = dot3(fh[...], fl[...], xh[...], xl[...])
+        for r in range(0, halo, 16):
+            block = ubuf[k, r : r + 16].astype(F32)
+            uf[k, r : r + 16] = block
+            uh[0, r : r + 16] = block
+        for r in range(0, taps + 16, 16):
+            xh[r : r + 16], xl[r : r + 16] = split(mixed(wv, delayed(uh, 0, r, 16)))
+        blank = jnp.zeros((tokens - taps - 16, chans), BF16)
+        xh[taps + 16 : tokens] = blank
+        xl[taps + 16 : tokens] = blank
+        qb[k, 0:16] = mixed(wg, delayed(uf, k, taps, 16))
+        vs[k] += dot3(fh[:, :tokens], fl[:, :tokens], xh[:tokens, :], xl[:tokens, :])
         spectrum_product(hs, k, vs, k, 1)
         zb[k] = dot3(ih[taps:, :], il[taps:, :], xh[...], xl[...])
 
@@ -245,81 +257,83 @@
 
     partner = ctx + 1 - 2 * core
 
-    for k in range(2):
+    def filter_part(k):
         finish(gbuf.at[k], a2a_recv.at[2 + k])
-        gate_sums = [jnp.zeros((8, chans), F32) for _ in range(3)]
         for r in range(0, tokens, 32):
             g = gbuf[k, r : r + 32].astype(F32)
             xh[taps + r : taps + r + 32], xl[taps + r : taps + r + 32] = split(
                 g * qb[k, r : r + 32]
             )
-            dq = g * zb[k, r : r + 32]
-            dqb[k, 16 + r : 48 + r] = dq
-            u = delayed(k, taps + r, 32)
-            gate_sums = [s + fold(dq * d) for s, d in zip(gate_sums, u)]
-        ds[0] = dot3(fh[:, taps:], fl[:, taps:], xh[taps:, :], xl[taps:, :])
-        spectrum_product(vs, k, ds, 0, -1)
-        part[0:taps] = dot3(ih[0:taps, :], il[0:taps, :], xh[...], xl[...]) * scale
-        if k == 1:
-            finish(part_in, one_recv.at[0])
-            for s in range(xs):
-                rows_of = slice(s * slice_rows, (s + 1) * slice_rows)
-                rs[s] = (part[rows_of] + part_in[rows_of]).astype(BF16)
-            loop(
-                xs,
-                lambda i: remote(
-                    rs.at[x_peer(i)], xr.at[x], one_send.at[1], one_recv.at[1],
-                    x_ctx(x_peer(i)), tp,
-                ).start(),
-            )
-            xr[x] = rs[x]
-        spectrum_product(hs, k, ds, 0, -1)
+            dqb[k, 16 + r : 48 + r] = g * zb[k, r : r + 32]
+        ds[k] = dot3(fh[:, taps:], fl[:, taps:], xh[taps:, :], xl[taps:, :])
+        spectrum_product(vs, k, ds, k, -1)
+        part[k] = dot3(ih[0:taps, :], il[0:taps, :], xh[...], xl[...]) * scale
+
+    def extra_part(k):
+        spectrum_product(hs, k, ds, k, -1)
         w1b[k, 16 : 16 + length] = dot3(ih[...], il[...], xh[...], xl[...])
-        value_sums = [jnp.zeros((8, chans), F32) for _ in range(3)]
+        sums = [jnp.zeros((8, chans), F32) for _ in range(6)]
         for r in range(0, length, 32):
+            u = delayed(uf, k, r, 32)
             w1 = w1b[k, 16 + r : 48 + r]
-            u = delayed(k, r, 32)
-            value_sums = [s + fold(w1 * d) for s, d in zip(value_sums, u)]
-        for i, s in enumerate(gate_sums + value_sums):
-            part[taps + i : taps + i + 1] = jnp.sum(s, axis=0, keepdims=True) * scale
-        part[taps + 6 : taps + 8] = jnp.zeros((2, chans), F32)
-        if k == 0:
-            sent = remote(part, part_in, one_send.at[0], one_recv.at[0], partner, tp)
-            sent.start()
-            input_gradient(k)
-            sent.wait_send()
-
-    own_extra = part[taps : taps + EXTRA] + part_in[taps : taps + EXTRA]
-    xe[x] = jnp.concatenate([own_extra[:, : chans // 2], own_extra[:, chans // 2 :]]).astype(BF16)
-    loop(
-        xs,
-        lambda i: remote(
-            xe.at[x], xe.at[x], one_send.at[4], one_recv.at[4], x_ctx(x_peer(i)), tp
-        ).start(),
-    )
+            if r >= taps:
+                dq = dqb[k, 16 + r - taps : 48 + r - taps]
+                sums[:3] = [s + fold(dq * d) for s, d in zip(sums[:3], u)]
+            sums[3:] = [s + fold(w1 * d) for s, d in zip(sums[3:], u)]
+        for i, s in enumerate(sums):
+            total = jnp.sum(s, axis=0, keepdims=True) * scale
+            for lane in range(2):
+                ep[k, 8 * lane + i : 8 * lane + i + 1] = total[
+                    :, lane * (chans // 2) : (lane + 1) * (chans // 2)
+                ]
+
+    ep[...] = jnp.zeros(ep.shape, F32)
+    uf[:, halo - 16 : halo] = jnp.zeros((2, 16, chans), F32)
+    uh[0, halo : halo + 16] = jnp.zeros((16, chans), F32)
+    own_spectrum(0)
+    own_spectrum(1)
+    halo_spectrum(0)
+    filter_part(0)
+    remote(part.at[0], part_in, one_send.at[0], one_recv.at[0], partner, tp).start()
+    halo_spectrum(1)
+    extra_part(0)
+    remote(ep.at[0], ep_in, one_send.at[7], one_recv.at[7], partner, tp).start()
+    filter_part(1)
+    finish(part_in, one_recv.at[0])
+    for s in range(xs):
+        rows_of = slice(s * slice_rows, (s + 1) * slice_rows)
+        rs[s] = (part[1, rows_of] + part_in[rows_of]).astype(BF16)
+    for d in x_order:
+        to = x_peer(d)
+        remote(rs.at[to], xr.at[x], one_send.at[1], one_recv.at[1], x_ctx(to), tp).start()
+    xr[x] = rs[x]
+    extra_part(1)
+    finish(ep_in, one_recv.at[7])
+    xe[x] = (ep[1] + ep_in[...]).astype(BF16)
+    for d in x_order:
+        remote(
+            xe.at[x], xe.at[x], one_send.at[4], one_recv.at[4], x_ctx(x_peer(d)), tp
+        ).start()
+    input_gradient(0)
     input_gradient(1)
     finish(xr.at[pl.ds(0, xs - 1)], one_recv.at[1])
     total = xr[0].astype(F32)
     for s in range(1, xs):
         total = total + xr[s].astype(F32)
     yr[ylo] = total
-    loop(
-        ys,
-        lambda i: remote(
+    for i in range(1, ys):
+        remote(
             yr.at[ylo], yr.at[ylo], one_send.at[2], one_recv.at[2], y_ctx(i), tp
-        ).start(),
-    )
+        ).start()
     finish(xe.at[pl.ds(0, xs - 1)], one_recv.at[4])
     total = xe[0].astype(F32)
     for s in range(1, xs):
         total = total + xe[s].astype(F32)
     ye[ylo] = total
-    loop(
-        ys,
-        lambda i: remote(
+    for i in range(1, ys):
+        remote(
             ye.at[ylo], ye.at[ylo], one_send.at[5], one_recv.at[5], y_ctx(i), tp
-        ).start(),
-    )
+        ).start()
 
     @pl.when(ctx < nctx - 1)
     def _():
@@ -340,12 +354,10 @@
         total = total + yr[s]
     slot = core * xs + x
     ag[slot] = total.astype(BF16)
-    loop(
-        2 * xs,
-        lambda i: remote(
-            ag.at[slot], ag.at[slot], one_send.at[3], one_recv.at[3], row_peer(i), tp
-        ).start(),
-    )
+    for step in row_order:
+        remote(
+            ag.at[slot], ag.at[slot], one_send.at[3], one_recv.at[3], row_peer(step), tp
+        ).start()
     finish(ye.at[pl.ds(0, ys - 1)], one_recv.at[5])
     total = ye[0]
     for s in range(1, ys):
@@ -387,6 +399,8 @@
     finish(xe.at[pl.ds(0, xs - 1)], one_send.at[4])
     finish(ye.at[pl.ds(0, ys - 1)], one_send.at[5])
     finish(ext, one_send.at[6])
+    finish(part_in, one_send.at[0])
+    finish(ep_in, one_send.at[7])
 
 
 def write_out(*refs):
@@ -422,7 +436,7 @@
         *[pltpu.VMEM((length, length), BF16) for _ in range(4)],
         pltpu.VMEM((2, length, chans), F32),
         pltpu.VMEM((2, length, chans), F32),
-        pltpu.VMEM((1, length, chans), F32),
+        pltpu.VMEM((2, length, chans), F32),
         pltpu.VMEM((2, halo + tokens, chans), F32),
         pltpu.VMEM((2, tokens, chans), F32),
         pltpu.VMEM((2, tokens, chans), F32),
@@ -433,8 +447,11 @@
         pltpu.VMEM((2, tokens, chans), F32),
         pltpu.VMEM((2, halo, chans), BF16),
         pltpu.VMEM((2, halo, chans), BF16),
-        pltpu.VMEM((taps + EXTRA, chans), F32),
-        pltpu.VMEM((taps + EXTRA, chans), F32),
+        pltpu.VMEM((1, halo + 16, chans), F32),
+        pltpu.VMEM((2, taps, chans), F32),
+        pltpu.VMEM((taps, chans), F32),
+        pltpu.VMEM((2, 2 * EXTRA, chans // 2), F32),
+        pltpu.VMEM((2 * EXTRA, chans // 2), F32),
         pltpu.VMEM((2 * EXTRA, chans // 2), F32),
         pltpu.VMEM((2 * EXTRA, chans // 2), F32),
         pltpu.VMEM((xs, slice_rows, chans), BF16),
@@ -452,8 +469,8 @@
         pltpu.SemaphoreType.DMA((2,)),
         pltpu.SemaphoreType.DMA((2,)),
         pltpu.SemaphoreType.DMA((8,)),
-        pltpu.SemaphoreType.DMA((7,)),
-        pltpu.SemaphoreType.DMA((7,)),
+        pltpu.SemaphoreType.DMA((8,)),
+        pltpu.SemaphoreType.DMA((8,)),
     ]
     results = pl.pallas_call(
         functools.partial(kernel, (nctx, ntp, xs, ys, taps, scale)),

time: 62.1 us -> 59.2 us (0.953)
  Pallas kernels: 59.8 us -> 56.9 us
    pallas_call x1, Pallas kernels: 59 us -> 56.1 us  [shards(): pl.pallas_call(functools.partial(kernel, (nctx, ntp, xs, ys, taps, scale)...]
where the time goes in v4:
time: 59.2 us; the launch traced here: 59 us
  Pallas kernels  56.9 us (96%)
  local copies, waits for them, and re-layouts  1.39 us (2%)
  between operations  0.65 us (1%)
    pallas_call x1, Pallas kernels, shards(): pl.pallas_call(functools.partial(kernel, (nctx, ntp, xs, ys, taps, scale)...  56.1 us
    unnamed x4, local copies, waits for them, and re-layouts  1.39 us

profile of v4, /device:TPU:1, one launch (start us, length us, event | category | flops | bytes accessed | tf_op | source)
XLA Modules:
  0.0 59.0 jit_solution(14758394361001430706)
XLA Ops:
  0.6 0.0 copy-start
  0.6 0.7 %copy-done = f32[3,512]{1,0:T(4,128)S(1)} copy-done((f32[3,512]{1,0:T(4,128)S(1)}, f32[3,512]{1,0:T(4,128)}, u32[]{:S(2)}) %copy-start) | copy-done | bytes 6168
  1.3 0.0 copy-start.1
  1.3 0.7 %copy-done.1 = f32[3,512]{1,0:T(4,128)S(1)} copy-done((f32[3,512]{1,0:T(4,128)S(1)}, f32[3,512]{1,0:T(4,128)}, u32[]{:S(2)}) %copy-start.1) | copy-done | bytes 6168
  2.0 56.1 %shard_map.120 = (bf16[256,512]{1,0:T(8,128)(2,1)S(1)}, f32[128,512]{1,0:T(8,128)S(1)}, f32[3,512]{1,0:T(4,128)S(1)}, f32[3,512]{1,0:T(4,128)S(1)}) custom-call(bf16[16,8192]{1,0:T(8,128)(2,1)} %og.1, bf16[16,8192]{1,0:T(8,128)(2,1)} %si.1, f32[128,512]{1,0:T(8,128)} %h_hbm.1, f32[3,512]{1,0:T(4,128)S(1)} %copy-done, f32[3,512]{1,0:T(4,128)S(1)} %copy-done.1, ...), custom_call_target="tpu_custom_call" | custom-call | tf_op jit(solution)/shard_map/pallas_call | solution.py:475
  58.1 0.8 %shard_map.121 = (bf16[256,512]{1,0:T(8,128)(2,1)}, f32[128,512]{1,0:T(8,128)}, f32[3,512]{1,0:T(4,128)}, f32[3,512]{1,0:T(4,128)}) custom-call(bf16[256,512]{1,0:T(8,128)(2,1)S(1)} %get-tuple-element.8.refs_0_, f32[128,512]{1,0:T(8,128)S(1)} %get-tuple-element.9.refs_1_, f32[3,512]{1,0:T(4,128)S(1)} %get-tuple-element.10.refs_2_, ...), custom_call_target="tpu_custom_call" | custom-call | tf_op jit(solution)/shard_map/pallas_call | solution.py:493
Async XLA Ops:
  0.6 0.7 %copy-start = (f32[3,512]{1,0:T(4,128)S(1)}, f32[3,512]{1,0:T(4,128)}, u32[]{:S(2)}) copy-start(f32[3,512]{1,0:T(4,128)} %gt_hbm.1) | copy-start | bytes 18436
  1.3 0.7 %copy-start.1 = (f32[3,512]{1,0:T(4,128)S(1)}, f32[3,512]{1,0:T(4,128)}, u32[]{:S(2)}) copy-start(f32[3,512]{1,0:T(4,128)} %w_hbm.1) | copy-start | bytes 18436

commit v5 on v4

--- a/solution.py
+++ b/solution.py
@@ -67,7 +67,11 @@
     ylo = ctx // (2 * xs)
     deep = ntp // 2
     tp_far = sorted(range(deep), key=lambda d: -min(d, deep - d))
-    tp_order = [(far, d) for d in tp_far for far in (1, 0) if far or d]
+    across, along = [(1, d) for d in tp_far], [(0, d) for d in tp_far if d]
+    tp_order = []
+    while across or along:
+        tp_order += across[:2] + along[:1]
+        across, along = across[2:], along[1:]
     x_order = sorted(range(1, xs), key=lambda d: -min(d, xs - d))
     row_order = [(d, c) for d in x_order for c in range(2)] + [(0, 1)]
 
@@ -99,7 +103,11 @@
         return (ylo * xs + other) * 2 + core
 
     def y_ctx(i):
-        return (lax.rem(ylo + i, ys) * xs + x) * 2 + core
+        low = ylo < ys // 2
+        pair = [jnp.where(low, ys - 1, 0), jnp.where(low, ys - 2, 1)]
+        other = ylo + 1 - 2 * lax.rem(ylo, 2)
+        to = [pair[0], pair[1], other][i - 1] if ys == 4 else lax.rem(ylo + i, ys)
+        return (to * xs + x) * 2 + core
 
     barrier = pltpu.get_barrier_semaphore()
 
@@ -296,8 +304,6 @@
     filter_part(0)
     remote(part.at[0], part_in, one_send.at[0], one_recv.at[0], partner, tp).start()
     halo_spectrum(1)
-    extra_part(0)
-    remote(ep.at[0], ep_in, one_send.at[7], one_recv.at[7], partner, tp).start()
     filter_part(1)
     finish(part_in, one_recv.at[0])
     for s in range(xs):
@@ -307,6 +313,8 @@
         to = x_peer(d)
         remote(rs.at[to], xr.at[x], one_send.at[1], one_recv.at[1], x_ctx(to), tp).start()
     xr[x] = rs[x]
+    extra_part(0)
+    remote(ep.at[0], ep_in, one_send.at[7], one_recv.at[7], partner, tp).start()
     extra_part(1)
     finish(ep_in, one_recv.at[7])
     xe[x] = (ep[1] + ep_in[...]).astype(BF16)
@@ -429,6 +437,8 @@
     matrices = [jnp.asarray(m) for m in transforms(length)]
     hbm = pl.BlockSpec(memory_space=pltpu.HBM)
     vmem = pl.BlockSpec(memory_space=pltpu.VMEM)
+    gate_taps = pltpu.with_memory_space_constraint(gate_taps, pltpu.HBM)
+    value_featurizer_weights = pltpu.with_memory_space_constraint(value_featurizer_weights, pltpu.HBM)
     scratch = [
         pltpu.VMEM((2, halo + tokens, chans), BF16),
         pltpu.VMEM((2, tokens, chans), BF16),

time: 59.2 us -> 58.2 us (0.983)
  local copies, waits for them, and re-layouts: 1.39 us -> 0 us
    unnamed x4 -> x0, local copies, waits for them, and re-layouts: 1.39 us -> none
where the time goes in v5:
time: 58.2 us; the launch traced here: 58.1 us
  Pallas kernels  57.4 us (99%)
  between operations  0.64 us (1%)
    pallas_call x1, Pallas kernels, shards(): pl.pallas_call(functools.partial(kernel, (nctx, ntp, xs, ys, taps, scale)...  56.6 us

profile of v5, /device:TPU:1, one launch (start us, length us, event | category | flops | bytes accessed | tf_op | source)
XLA Modules:
  0.0 58.1 jit_solution(15442314843943469875)
XLA Ops:
  0.6 56.6 %shard_map.120 = (bf16[256,512]{1,0:T(8,128)(2,1)S(1)}, f32[128,512]{1,0:T(8,128)S(1)}, f32[3,512]{1,0:T(4,128)S(1)}, f32[3,512]{1,0:T(4,128)S(1)}) custom-call(bf16[16,8192]{1,0:T(8,128)(2,1)} %og.1, bf16[16,8192]{1,0:T(8,128)(2,1)} %si.1, f32[128,512]{1,0:T(8,128)} %h_hbm.1, f32[3,512]{1,0:T(4,128)} %gt_hbm.1, f32[3,512]{1,0:T(4,128)} %w_hbm.1, ...), custom_call_target="tpu_custom_call" | custom-call | tf_op jit(solution)/shard_map/pallas_call | solution.py:485
  57.3 0.8 %shard_map.121 = (bf16[256,512]{1,0:T(8,128)(2,1)}, f32[128,512]{1,0:T(8,128)}, f32[3,512]{1,0:T(4,128)}, f32[3,512]{1,0:T(4,128)}) custom-call(bf16[256,512]{1,0:T(8,128)(2,1)S(1)} %get-tuple-element.8.refs_0_, f32[128,512]{1,0:T(8,128)S(1)} %get-tuple-element.9.refs_1_, f32[3,512]{1,0:T(4,128)S(1)} %get-tuple-element.10.refs_2_, ...), custom_call_target="tpu_custom_call" | custom-call | tf_op jit(solution)/shard_map/pallas_call | solution.py:503

commit v6 on v4

--- a/solution.py
+++ b/solution.py
@@ -99,7 +99,11 @@
         return (ylo * xs + other) * 2 + core
 
     def y_ctx(i):
-        return (lax.rem(ylo + i, ys) * xs + x) * 2 + core
+        low = ylo < ys // 2
+        pair = [jnp.where(low, ys - 1, 0), jnp.where(low, ys - 2, 1)]
+        other = ylo + 1 - 2 * lax.rem(ylo, 2)
+        to = [pair[0], pair[1], other][i - 1] if ys == 4 else lax.rem(ylo + i, ys)
+        return (to * xs + x) * 2 + core
 
     barrier = pltpu.get_barrier_semaphore()
 
@@ -374,33 +378,33 @@
     put_extra(ext, 1)
     finish(ext_in, one_recv.at[6])
     put_extra(ext_in, 0)
+    for k in range(2):
+        finish(ubuf.at[k, pl.ds(0, rows * (ntp - 1)), :], a2a_send.at[k])
+        finish(gbuf.at[k, pl.ds(0, rows * (ntp - 1)), :], a2a_send.at[2 + k])
+
+        @pl.when(ctx < nctx - 1)
+        def _(k=k):
+            finish(ubuf.at[k, pl.ds(0, halo), :], halo_send.at[k])
+
+        @pl.when(ctx > 0)
+        def _(k=k):
+            finish(head.at[k], head_send.at[k])
+
+    finish(rs.at[pl.ds(0, xs - 1)], one_send.at[1])
+    finish(yr.at[pl.ds(0, ys - 1)], one_send.at[2])
+    finish(xe.at[pl.ds(0, xs - 1)], one_send.at[4])
+    finish(ye.at[pl.ds(0, ys - 1)], one_send.at[5])
+    finish(ext, one_send.at[6])
+    finish(part_in, one_send.at[0])
+    finish(ep_in, one_send.at[7])
+
     finish(ag.at[pl.ds(0, 2 * xs - 1)], one_recv.at[3])
     for half in range(2):
         for s in range(xs):
             efg_out[
                 s * slice_rows : (s + 1) * slice_rows, half * chans : (half + 1) * chans
             ] = ag[half * xs + s].astype(F32)
-
-    for k in range(2):
-        finish(ubuf.at[k, pl.ds(0, rows * (ntp - 1)), :], a2a_send.at[k])
-        finish(gbuf.at[k, pl.ds(0, rows * (ntp - 1)), :], a2a_send.at[2 + k])
-
-        @pl.when(ctx < nctx - 1)
-        def _(k=k):
-            finish(ubuf.at[k, pl.ds(0, halo), :], halo_send.at[k])
-
-        @pl.when(ctx > 0)
-        def _(k=k):
-            finish(head.at[k], head_send.at[k])
-
-    finish(rs.at[pl.ds(0, xs - 1)], one_send.at[1])
-    finish(yr.at[pl.ds(0, ys - 1)], one_send.at[2])
     finish(ag.at[pl.ds(0, 2 * xs - 1)], one_send.at[3])
-    finish(xe.at[pl.ds(0, xs - 1)], one_send.at[4])
-    finish(ye.at[pl.ds(0, ys - 1)], one_send.at[5])
-    finish(ext, one_send.at[6])
-    finish(part_in, one_send.at[0])
-    finish(ep_in, one_send.at[7])
 
 
 def write_out(*refs):
@@ -429,6 +433,8 @@
     matrices = [jnp.asarray(m) for m in transforms(length)]
     hbm = pl.BlockSpec(memory_space=pltpu.HBM)
     vmem = pl.BlockSpec(memory_space=pltpu.VMEM)
+    gate_taps = pltpu.with_memory_space_constraint(gate_taps, pltpu.HBM)
+    value_featurizer_weights = pltpu.with_memory_space_constraint(value_featurizer_weights, pltpu.HBM)
     scratch = [
         pltpu.VMEM((2, halo + tokens, chans), BF16),
         pltpu.VMEM((2, tokens, chans), BF16),

time: 59.2 us -> 57.6 us (0.973)
  local copies, waits for them, and re-layouts: 1.39 us -> 0 us
    unnamed x4 -> x0, local copies, waits for them, and re-layouts: 1.39 us -> none
where the time goes in v6:
time: 57.6 us; the launch traced here: 57.5 us
  Pallas kernels  56.8 us (99%)
  between operations  0.64 us (1%)
    pallas_call x1, Pallas kernels, shards(): pl.pallas_call(functools.partial(kernel, (nctx, ntp, xs, ys, taps, scale)...  56 us

profile of v6, /device:TPU:1, one launch (start us, length us, event | category | flops | bytes accessed | tf_op | source)
XLA Modules:
  0.0 57.5 jit_solution(1883043518168743159)
XLA Ops:
  0.6 56.0 %shard_map.120 = (bf16[256,512]{1,0:T(8,128)(2,1)S(1)}, f32[128,512]{1,0:T(8,128)S(1)}, f32[3,512]{1,0:T(4,128)S(1)}, f32[3,512]{1,0:T(4,128)S(1)}) custom-call(bf16[16,8192]{1,0:T(8,128)(2,1)} %og.1, bf16[16,8192]{1,0:T(8,128)(2,1)} %si.1, f32[128,512]{1,0:T(8,128)} %h_hbm.1, f32[3,512]{1,0:T(4,128)} %gt_hbm.1, f32[3,512]{1,0:T(4,128)} %w_hbm.1, ...), custom_call_target="tpu_custom_call" | custom-call | tf_op jit(solution)/shard_map/pallas_call | solution.py:481
  56.7 0.8 %shard_map.121 = (bf16[256,512]{1,0:T(8,128)(2,1)}, f32[128,512]{1,0:T(8,128)}, f32[3,512]{1,0:T(4,128)}, f32[3,512]{1,0:T(4,128)}) custom-call(bf16[256,512]{1,0:T(8,128)(2,1)S(1)} %get-tuple-element.8.refs_0_, f32[128,512]{1,0:T(8,128)S(1)} %get-tuple-element.9.refs_1_, f32[3,512]{1,0:T(4,128)S(1)} %get-tuple-element.10.refs_2_, ...), custom_call_target="tpu_custom_call" | custom-call | tf_op jit(solution)/shard_map/pallas_call | solution.py:499
